TPU v7x, 128 devices: a whole 4x4x4 slice. The times are simulated.
128 devices in a mesh: seq: 4 (over y_hi, core), fsdp: 32 (over z, x, y_lo).
Axes of the slice: x: 4, y: 4 (y_hi: 2, y_lo: 2; y = y_hi * 2 + y_lo), z: 4, core: 2. Of those that a mesh axis runs over, the one named last changes fastest.
Arguments:
- hidden_in: bfloat16 [2048, 16384], P('seq', 'fsdp'), may hold values from -6 to 6
- gain_in: float32 [16384], P('fsdp'), may hold values from 0.25 to 1.75
- w_query: bfloat16 [16384, 4096], P('fsdp'), may hold values from -0.046875 to 0.046875
- query_scale: float32 [4096], replicated, may hold values from 0.5 to 2
- w_key: bfloat16 [16384, 256], P('fsdp'), may hold values from -0.046875 to 0.046875
- key_scale: float32 [256], replicated, may hold values from 0.5 to 2
- w_value: bfloat16 [16384, 256], P('fsdp'), may hold values from -0.046875 to 0.046875
- value_scale: float32 [256], replicated, may hold values from 0.5 to 2
- w_out: bfloat16 [4096, 16384], P(None, 'fsdp'), may hold values from -0.125 to 0.125
- out_scale: float32 [16384], P('fsdp'), may hold values from 0.5 to 2
- gain_mid: float32 [16384], P('fsdp'), may hold values from 0.25 to 1.75
- head_order: int32 [32], replicated, may hold values from 0 to 31, each once
Outputs:
- hessian: float32 [16384, 16384], P('fsdp', 'seq')
- residual_out: bfloat16 [2048, 16384], P('seq', 'fsdp')
All inputs are finite; a program needn't handle non-finite values.
Results may differ from a plain program's by a relative error of at most 0.009.
Values may be sent and summed in bfloat16 or wider, within the bound.
No kernel may reach another device: no remote copies, remote signals or barrier semaphores. Data moves between devices by JAX's collectives and lax.ppermute only.
A program may use at most 128 MiB of HBM per device.

v0:
```python
import jax
import jax.numpy as jnp
from jax import lax
from jax.sharding import PartitionSpec as P

D = 16384
HEAD = 128
GROUP = 16
KVW = 2
L = 256
KEEP = 16
epsilon = 1e-05


def sent_to_all(array, axis):
    copies = jnp.broadcast_to(array, (lax.axis_size(axis), *array.shape))
    return lax.all_to_all(copies, axis, split_axis=0, concat_axis=0, tiled=True)


def over_copies(array, axis):
    return sent_to_all(array, axis).sum(axis=0)


def in_order(pieces, dim):
    pieces = jnp.moveaxis(pieces, 0, dim)
    shape = pieces.shape
    return pieces.reshape(*shape[:dim], shape[dim] * shape[dim + 1], *shape[dim + 2 :])


def gather_directly(array, axis, dim):
    pieces = sent_to_all(array, axis)
    return in_order(pieces, dim)


def rotate(values_in, positions):
    half_size = values_in.shape[-1] // 2
    steps_idx = jnp.arange(half_size, dtype=jnp.float32)
    frequency = jnp.exp(-jnp.log(jnp.float32(500000.0)) * steps_idx * 2.0 / values_in.shape[-1])
    angles = positions.astype(jnp.float32)[:, None] * frequency[None, :]
    cosine = jnp.cos(angles)[:, None, :]
    sine = jnp.sin(angles)[:, None, :]
    first_half = values_in[..., :half_size]
    second_half = values_in[..., half_size:]
    return jnp.concatenate(
        [first_half * cosine - second_half * sine, second_half * cosine + first_half * sine],
        axis=-1,
    )


def shards(
    hidden_in,
    gain_in,
    w_query,
    query_scale,
    w_key,
    key_scale,
    w_value,
    value_scale,
    w_out,
    out_scale,
    gain_mid,
    head_order,
):
    group_tok = hidden_in.shape[0]
    shard_count = lax.axis_size("fsdp")
    seq_count = lax.axis_size("seq")
    row_count = group_tok // shard_count
    first_row = lax.axis_index("fsdp") * row_count
    kv_width = w_key.shape[1]
    hidden_f = hidden_in.astype(jnp.float32)
    square_sum = over_copies(jnp.sum(hidden_f * hidden_f, axis=1), "fsdp")
    inverse = lax.rsqrt(square_sum / D + epsilon)
    normed = (hidden_f * inverse[:, None] * gain_in[None, :]).astype(jnp.bfloat16)
    kept_heads = head_order[:KEEP]
    head_cols = (kept_heads[:, None] * HEAD + jnp.arange(HEAD, dtype=jnp.int32)[None, :]).reshape(
        -1
    )
    kv_weight = jnp.concatenate([w_key, w_value], axis=1)
    kv_scales = jnp.concatenate([key_scale, value_scale])
    my_positions = (first_row + jnp.arange(row_count, dtype=jnp.int32)) % L
    query_w = jnp.take(w_query, head_cols, axis=1)
    query_sc = jnp.take(query_scale, head_cols)
    query_width = query_w.shape[1]
    joint_w = jnp.concatenate([query_w, kv_weight], axis=1)
    summed = lax.psum_scatter(
        jnp.dot(normed, joint_w, preferred_element_type=jnp.float32),
        "fsdp",
        scatter_dimension=0,
        tiled=True,
    )
    query_rows = summed[:, :query_width] * query_sc[None, :]
    kv_summed = summed[:, query_width:]
    count_rows = kv_summed.shape[0]
    kv_scaled = kv_summed * kv_scales[None, :]
    key_rot = rotate(kv_scaled[:, :kv_width].reshape(count_rows, KVW, HEAD), my_positions).astype(
        jnp.bfloat16
    )
    value_part = kv_scaled[:, kv_width:].astype(jnp.bfloat16)
    kv_local = jnp.concatenate([key_rot.reshape(count_rows, kv_width), value_part], axis=1)
    kv_group = gather_directly(kv_local, "fsdp", 0)
    query_rot = rotate(query_rows.reshape(row_count, KEEP, HEAD), my_positions).astype(jnp.bfloat16)
    seq_start = first_row // L * L
    kv_seq = lax.dynamic_slice_in_dim(kv_group, seq_start, L, 0)
    key_seq = kv_seq[:, :kv_width].reshape(L, KVW, HEAD)
    value_seq = kv_seq[:, kv_width:].reshape(L, KVW, HEAD)
    select = ((kept_heads // GROUP)[:, None] == jnp.arange(KVW, dtype=jnp.int32)[None, :]).astype(
        jnp.bfloat16
    )
    key_heads = jnp.einsum(
        "lgd,hg->lhd", key_seq, select, preferred_element_type=jnp.float32
    ).astype(jnp.bfloat16)
    value_heads = jnp.einsum(
        "lgd,hg->lhd", value_seq, select, preferred_element_type=jnp.float32
    ).astype(jnp.bfloat16)
    scale_factor = 1.0 / jnp.sqrt(jnp.float32(HEAD))
    scores = (
        jnp.einsum("qhd,lhd->hql", query_rot, key_heads, preferred_element_type=jnp.float32)
        * scale_factor
    )
    causal = jnp.arange(L, dtype=jnp.int32)[None, :] <= my_positions[:, None]
    scores = jnp.where(causal[None], scores, -1e30)
    weights = jax.nn.softmax(scores, axis=-1).astype(jnp.bfloat16)
    attended = jnp.einsum("hql,lhd->qhd", weights, value_heads, preferred_element_type=jnp.float32)
    attended = attended.astype(jnp.bfloat16).reshape(row_count, KEEP * HEAD)
    out_w = jnp.take(w_out, head_cols, axis=0)
    mixed = (
        jnp.dot(gather_directly(attended, "fsdp", 0), out_w, preferred_element_type=jnp.float32)
        * out_scale[None, :]
    )
    residual_out = (hidden_f + mixed).astype(jnp.bfloat16)
    resid_f = residual_out.astype(jnp.float32)
    square_mid = over_copies(jnp.sum(resid_f * resid_f, axis=1), "fsdp")
    inverse_mid = lax.rsqrt(square_mid / D + epsilon)
    ffn_input = (resid_f * inverse_mid[:, None] * gain_mid[None, :]).astype(jnp.bfloat16)
    local_width = ffn_input.shape[1]
    rows_whole = gather_directly(ffn_input, "seq", 0)
    rows_whole = rows_whole.reshape(seq_count, shard_count, row_count, local_width)
    rows_whole = rows_whole.transpose(1, 0, 2, 3).reshape(seq_count * group_tok, local_width)
    relayed = lax.all_to_all(
        lax.all_to_all(ffn_input, "fsdp", split_axis=0, concat_axis=1, tiled=True),
        "seq",
        split_axis=1,
        concat_axis=0,
        tiled=True,
    )
    columns_whole = lax.all_gather(relayed, "fsdp", axis=0, tiled=True)
    tile_sum = lax.dot_general(
        rows_whole, columns_whole, (((0,), (0,)), ((), ())), preferred_element_type=jnp.float32
    )
    hessian = tile_sum / (seq_count * group_tok)
    return (hessian, residual_out)


def solution(mesh):
    return jax.shard_map(
        shards,
        mesh=mesh,
        in_specs=(
            P("seq", "fsdp"),
            P("fsdp"),
            P("fsdp", None),
            P(),
            P("fsdp", None),
            P(),
            P("fsdp", None),
            P(),
            P(None, "fsdp"),
            P("fsdp"),
            P("fsdp"),
            P(),
        ),
        out_specs=(P("fsdp", "seq"), P("seq", "fsdp")),
        check_vma=False,
    )
```

profile of v0, /device:TPU:24, one launch (start us, length us, event | category | flops | bytes accessed | tf_op | source)
XLA Modules:
  0.0 713.6 jit_solution(760770537415510053)
XLA Ops:
  7.2 0.0 copy-start
  7.2 1.2 fusion.27
  8.4 0.7 broadcast_in_dim.48
  9.1 9.4 %all-to-all-start = ((f32[32,1,512]{2,1,0:T(1,128)}), f32[32,1,512]{2,1,0:T(1,128)S(1)}, u32[]{:S(2)}, u32[]{:S(2)}) async-start(f32[32,1,512]{2,1,0:T(1,128)} %broadcast_in_dim.48), calls=%async_computation | async-start | bytes 131072 | tf_op jit(solution)/shard_map/all_to_all | solution.py:17
  18.5 0.0 reduce-scatter.2.cloned.1.call-start
  18.5 0.7 and_select_fusion.1
  19.2 0.1 compare_and_fusion
  19.3 0.1 iota_add_fusion
  19.4 6.4 copy.61
  25.8 10.3 %gather_fusion = bf16[2048,512]{1,0:T(8,128)(2,1)S(1)} fusion(bf16[512,4096]{0,1:T(8,128)(2,1)} %copy.61, s32[2048]{0:T(1024)S(1)} %broadcast_clamp_fusion), kind=kCustom, calls=%fused_computation | custom fusion | bytes 4202496 | tf_op jit(solution)/shard_map/jit(_take)/gather | solution.py:81
  36.1 0.0 copy-start.4
  36.1 0.0 copy-start.5
  36.1 0.0 copy-start.2
  36.1 0.0 copy-start.9
  36.2 1.6 select_bitcast_fusion
  37.7 0.1 copy.62
  37.9 0.1 copy.63
  38.0 0.0 all-to-all-done
  38.0 0.1 reduce_sum.46
  38.1 5.5 fusion.1
  43.7 0.0 reduce-scatter.2.cloned.1.call-update
  43.7 0.0 copy-done
  43.7 0.0 copy-start.7
  43.7 0.0 copy-start.8
  43.7 11.8 %gather_fusion.1 = f32[2048]{0:T(1024)S(1)} fusion(f32[4096]{0:T(1024)S(1)} %copy-done, s32[2048]{0:T(1024)S(1)} %broadcast_clamp_fusion), kind=kCustom, calls=%fused_computation.1 | custom fusion | bytes 24576 | tf_op jit(solution)/shard_map/jit(_take)/gather | solution.py:82
  55.6 0.1 iota_compare_fusion
  55.7 0.1 broadcast_select_fusion
  55.7 0.1 multiply_cosine_fusion
  55.9 159.8 %reduce-scatter.2.cloned.1.call-done = f32[16,2560]{1,0:T(8,128)} async-done(((f32[512,2560]{1,0:T(8,128)}), f32[16,2560]{1,0:T(8,128)}) %reduce-scatter.2.cloned.1.call-update) | async-done | bytes 163856 | tf_op jit(solution)/shard_map/reduce_scatter | solution.py:85
  215.7 0.8 slice_multiply_fusion.1
  216.5 0.1 subtract_convert_fusion.1
  216.6 0.1 pad_maximum_fusion.1
  216.7 0.9 broadcast_in_dim.51
  217.6 7.7 %all-to-all-start.1 = ((bf16[32,16,512]{2,1,0:T(8,128)(2,1)}), bf16[32,16,512]{2,1,0:T(8,128)(2,1)S(1)}, u32[]{:S(2)}, u32[]{:S(2)}) async-start(bf16[32,16,512]{2,1,0:T(8,128)(2,1)} %broadcast_in_dim.51), calls=%async_computation.2 | async-start | bytes 1048576 | tf_op jit(solution)/shard_map/all_to_all | solution.py:17
  225.2 0.9 fusion.36
  226.2 0.1 fusion.50
  226.3 0.1 subtract_convert_fusion
  226.4 11.5 %all-to-all-done.1 = bf16[32,16,512]{2,1,0:T(8,128)(2,1)S(1)} async-done(((bf16[32,16,512]{2,1,0:T(8,128)(2,1)}), bf16[32,16,512]{2,1,0:T(8,128)(2,1)S(1)}, u32[]{:S(2)}, u32[]{:S(2)}) %all-to-all-start.1) | async-done | bytes 524320 | tf_op jit(solution)/shard_map/all_to_all | solution.py:17
  238.0 0.5 fusion.10
  238.5 0.5 fusion.11
  239.0 0.6 fusion.51
  239.6 0.4 fusion.23
  240.0 1.6 broadcast_in_dim.84
  241.6 6.3 all-to-all-start.2
  247.9 0.0 copy-start.10
  247.9 0.0 all-gather.2.cloned.1.call-start
  247.9 10.3 %gather_fusion.2 = bf16[2048,512]{1,0:T(8,128)(2,1)S(1)} fusion(bf16[4096,512]{1,0:T(8,128)(2,1)} %param.20, s32[2048]{0:T(1024)S(1)} %broadcast_clamp_fusion), kind=kCustom, calls=%fused_computation.2 | custom fusion | bytes 4202496 | tf_op jit(solution)/shard_map/jit(_take)/gather | solution.py:125
  258.2 7.8 %all-to-all-done.2 = bf16[32,16,2048]{2,1,0:T(8,128)(2,1)} async-done(((bf16[32,16,2048]{2,1,0:T(8,128)(2,1)}), bf16[32,16,2048]{2,1,0:T(8,128)(2,1)}, u32[]{:S(2)}, u32[]{:S(2)}) %all-to-all-start.2) | async-done | bytes 2097184 | tf_op jit(solution)/shard_map/all_to_all | solution.py:17
  266.1 3.1 fusion.24
  269.2 13.7 %all_to_all.62 = f32[32,1,512]{2,1,0:T(1,128)S(1)} all-to-all(f32[32,1,512]{2,1,0:T(1,128)S(1)} %broadcast_in_dim.87), channel_id=1, replica_groups=mesh['seq'=4,'fsdp'=32] {'fsdp'}, dimensions={0} | all-to-all | bytes 131072 | tf_op jit(solution)/shard_map/all_to_all | solution.py:17
  282.9 0.1 reduce_sum.49
  283.0 0.2 fusion.26
  283.2 13.9 %all_to_all.63 = bf16[32,16,512]{2,1,0:T(8,128)(2,1)S(1)} all-to-all(bf16[32,16,512]{2,1,0:T(8,128)(2,1)S(1)} %bitcast.49), channel_id=1, replica_groups=mesh['seq'=4,'fsdp'=32] {'fsdp'}, dimensions={0} | all-to-all | bytes 1048576 | tf_op jit(solution)/shard_map/all_to_all | solution.py:140
  297.1 0.3 copy.71
  297.4 0.4 all_to_all.51
  297.8 0.0 copy-done.3
  297.8 0.3 copy.72
  298.1 11.9 %all_to_all.64 = bf16[16,4,4096]{2,0,1:T(8,128)(2,1)} all-to-all(bf16[16,4,4096]{2,0,1:T(8,128)(2,1)S(1)} %copy.72), channel_id=1, replica_groups=mesh['seq'=4,'fsdp'=32] {'seq'}, dimensions={1} | all-to-all | bytes 1048576 | tf_op jit(solution)/shard_map/all_to_all | solution.py:139
  310.0 0.0 all-gather.2.cloned.1.call-update
  310.0 0.2 broadcast_in_dim.88
  310.2 74.8 %all_to_all.65 = bf16[4,512,512]{2,1,0:T(8,128)(2,1)S(1)} all-to-all(bf16[4,512,512]{2,1,0:T(8,128)(2,1)S(1)} %broadcast_in_dim.88), channel_id=1, replica_groups=mesh['seq'=4,'fsdp'=32] {'seq'}, dimensions={0} | all-to-all | bytes 4194304 | tf_op jit(solution)/shard_map/all_to_all | solution.py:17
  385.0 0.2 copy.70
  385.2 307.0 %all-gather.2.cloned.1.call-done = bf16[2048,4096]{1,0:T(8,128)(2,1)} async-done(((bf16[64,4096]{1,0:T(8,128)(2,1)}), bf16[2048,4096]{1,0:T(8,128)(2,1)}) %all-gather.2.cloned.1.call-update) | async-done | bytes 16777232 | tf_op jit(solution)/shard_map/all_gather | solution.py:146
  692.2 14.6 %convolution_multiply_fusion = f32[512,4096]{1,0:T(8,128)} fusion(bf16[2048,512]{1,0:T(8,128)(2,1)S(1)} %bitcast.50, bf16[2048,4096]{1,0:T(8,128)(2,1)} %all-gather.2.cloned.1.call-done), kind=kOutput, calls=%fused_computation.4 | convolution fusion | flops 8592031744 | bytes 27262976 | tf_op jit(solution)/shard_map/dot_general | solution.py:147
  (30 shorter events, 0.3 us)
Async XLA Ops:
  7.2 36.5 %copy-start = (f32[4096]{0:T(1024)S(1)}, f32[4096]{0:T(1024)}, u32[]{:S(2)}) copy-start(f32[4096]{0:T(1024)} %param.15) | copy-start | bytes 49156
  9.1 28.9 %all-to-all-start = ((f32[32,1,512]{2,1,0:T(1,128)}), f32[32,1,512]{2,1,0:T(1,128)S(1)}, u32[]{:S(2)}, u32[]{:S(2)}) async-start(f32[32,1,512]{2,1,0:T(1,128)} %broadcast_in_dim.48), calls=%async_computation | async-start | bytes 131072 | tf_op jit(solution)/shard_map/all_to_all | solution.py:17
  18.5 197.2 %reduce-scatter.2.cloned.1.call-start = ((), (), s32[]{:S(2)}) async-start(), calls=%async_computation.8 | async-start | bytes 5406720 | tf_op jit(solution)/shard_map/reduce_scatter | solution.py:85
  36.1 1.6 copy-start.4
  36.1 1.7 copy-start.5
  36.1 2.0 copy-start.2
  36.1 2.0 copy-start.9
  43.7 11.9 %copy-start.7 = (f32[256]{0:T(256)S(1)}, f32[256]{0:T(256)}, u32[]{:S(2)}) copy-start(f32[256]{0:T(256)} %param.19) | copy-start | bytes 3076
  43.7 11.9 %copy-start.8 = (f32[256]{0:T(256)S(1)}, f32[256]{0:T(256)}, u32[]{:S(2)}) copy-start(f32[256]{0:T(256)} %param.17) | copy-start | bytes 3076
  217.6 20.3 %all-to-all-start.1 = ((bf16[32,16,512]{2,1,0:T(8,128)(2,1)}), bf16[32,16,512]{2,1,0:T(8,128)(2,1)S(1)}, u32[]{:S(2)}, u32[]{:S(2)}) async-start(bf16[32,16,512]{2,1,0:T(8,128)(2,1)} %broadcast_in_dim.51), calls=%async_computation.2 | async-start | bytes 1048576 | tf_op jit(solution)/shard_map/all_to_all | solution.py:17
  241.6 24.5 %all-to-all-start.2 = ((bf16[32,16,2048]{2,1,0:T(8,128)(2,1)}), bf16[32,16,2048]{2,1,0:T(8,128)(2,1)}, u32[]{:S(2)}, u32[]{:S(2)}) async-start(bf16[32,16,2048]{2,1,0:T(8,128)(2,1)} %broadcast_in_dim.84), calls=%async_computation.3 | async-start | bytes 4194304 | tf_op jit(solution)/shard_map/all_to_all | solution.py:17
  247.9 18.2 %copy-start.10 = (f32[512]{0:T(512)S(1)}, f32[512]{0:T(512)}, u32[]{:S(2)}) copy-start(f32[512]{0:T(512)} %param.21) | copy-start | bytes 6148
  247.9 444.4 %all-gather.2.cloned.1.call-start = ((), (), s32[]{:S(2)}) async-start(), calls=%async_computation.9 | async-start | bytes 17301504 | tf_op jit(solution)/shard_map/all_gather | solution.py:146
  266.1 16.9 %copy-start.6 = (f32[512]{0:T(512)S(1)}, f32[512]{0:T(512)}, u32[]{:S(2)}) copy-start(f32[512]{0:T(512)} %param.22) | copy-start | bytes 6148
  269.1 28.7 %copy-start.3 = (bf16[512,512]{1,0:T(8,128)(2,1)}, bf16[512,512]{1,0:T(8,128)(2,1)S(1)}, u32[]{:S(2)}) copy-start(bf16[512,512]{1,0:T(8,128)(2,1)S(1)} %get-tuple-element.17) | copy-start | bytes 1572868
  692.2 14.6 %copy-start.1 = (f32[4096]{0:T(1024)S(1)}, f32[4096]{0:T(1024)}, u32[]{:S(2)}) copy-start(f32[4096]{0:T(1024)} %param.15) | copy-start | bytes 49156
Sparse Core Ops, SparseCore 0:
  43.8 171.8 reduce-scatter.1
  310.1 382.0 all-gather.1
where the time goes:
time: 715 us; the launch traced here: 714 us
  waiting for transfers between devices  486 us (68%)
  blocking collectives  114 us (16%)
  local copies, waits for them, and re-layouts  43.9 us (6%)
  matrix products  25.2 us (4%)
  starting transfers between devices  23.4 us (3%)
  between operations  14.4 us (2%)
    all_gather x1, waiting for transfers between devices, shards(): columns_whole = lax.all_gather(relayed, 'fsdp', axis=0, tiled=True)  307 us
    reduce_scatter x1, waiting for transfers between devices, shards(): lax.psum_scatter(jnp.dot(normed, joint_w, preferred_element_type=jnp.floa...  160 us
    all_to_all x2, blocking collectives, sent_to_all(): return lax.all_to_all(copies, axis, split_axis=0, concat_axis=0, tiled=True)  88.6 us
    all_to_all x3, starting transfers between devices, sent_to_all(): return lax.all_to_all(copies, axis, split_axis=0, concat_axis=0, tiled=True)  23.4 us
    all_to_all x3, waiting for transfers between devices, sent_to_all(): return lax.all_to_all(copies, axis, split_axis=0, concat_axis=0, tiled=True)  19.3 us
    dot_general x1, matrix products, shards(): lax.dot_general(rows_whole, columns_whole, (((0,), (0,)), ((), ())), pref...  14.6 us
  transfers between devices with their start and end apart: 5, of which 4 were waited for; matrix products, arithmetic and copies ran while one was open for 6% of the time, Pallas kernels for 0%

commit v1 on v0

--- a/solution.py
+++ b/solution.py
@@ -143,7 +143,9 @@
         concat_axis=0,
         tiled=True,
     )
-    columns_whole = lax.all_gather(relayed, "fsdp", axis=0, tiled=True)
+    columns_whole = jnp.concatenate(
+        lax.all_to_all(jnp.stack([relayed] * lax.axis_size("fsdp")), "fsdp", 0, 0), axis=0
+    )
     tile_sum = lax.dot_general(
         rows_whole, columns_whole, (((0,), (0,)), ((), ())), preferred_element_type=jnp.float32
     )

time: 715 us -> 660 us (0.923)
  blocking collectives: 114 us -> 69.1 us
  waiting for transfers between devices: 486 us -> 461 us
  local copies, waits for them, and re-layouts: 43.9 us -> 51.2 us
    all_gather x1 -> x0, waiting for transfers between devices: 307 us -> none  [shards(): columns_whole = lax.all_gather(relayed, 'fsdp', axis=0, tiled=True)]
    all_to_all x0 -> x1, waiting for transfers between devices: none -> 281 us  [shards(): lax.all_to_all(jnp.stack([relayed] * lax.axis_size('fsdp')), 'fsdp', 0, 0)]
    all_to_all x2, blocking collectives: 88.6 us -> 43.4 us  [sent_to_all(): return lax.all_to_all(copies, axis, split_axis=0, concat_axis=0, tiled=True)]
  transfers between devices with their start and end apart: 5 -> 5, of which waited for: 4 -> 4; matrix products, arithmetic and copies ran while one was open for 6% -> 7% of each run, Pallas kernels for 0% -> 0%
where the time goes in v1:
time: 660 us; the launch traced here: 657 us
  waiting for transfers between devices  461 us (70%)
  blocking collectives  69.1 us (10%)
  local copies, waits for them, and re-layouts  51.2 us (8%)
  starting transfers between devices  29.8 us (5%)
  matrix products  25.7 us (4%)
  between operations  14.4 us (2%)
    all_to_all x1, waiting for transfers between devices, shards(): lax.all_to_all(jnp.stack([relayed] * lax.axis_size('fsdp')), 'fsdp', 0, 0)  281 us
    reduce_scatter x1, waiting for transfers between devices, shards(): lax.psum_scatter(jnp.dot(normed, joint_w, preferred_element_type=jnp.floa...  160 us
    all_to_all x2, blocking collectives, sent_to_all(): return lax.all_to_all(copies, axis, split_axis=0, concat_axis=0, tiled=True)  43.4 us
    all_to_all x3, starting transfers between devices, sent_to_all(): return lax.all_to_all(copies, axis, split_axis=0, concat_axis=0, tiled=True)  23.2 us
    all_to_all x3, waiting for transfers between devices, sent_to_all(): return lax.all_to_all(copies, axis, split_axis=0, concat_axis=0, tiled=True)  19.7 us
    dot_general x1, matrix products, shards(): lax.dot_general(rows_whole, columns_whole, (((0,), (0,)), ((), ())), pref...  15.2 us
    all_to_all x1, blocking collectives, shards(): lax.all_to_all(ffn_input, 'fsdp', split_axis=0, concat_axis=1, tiled=True)  13.9 us
  transfers between devices with their start and end apart: 5, of which 4 were waited for; matrix products, arithmetic and copies ran while one was open for 7% of the time, Pallas kernels for 0%

profile of v1, /device:TPU:24, one launch (start us, length us, event | category | flops | bytes accessed | tf_op | source)
XLA Modules:
  0.0 657.2 jit_solution(4919645649832026758)
XLA Ops:
  7.2 0.0 copy-start
  7.2 1.2 fusion.27
  8.4 0.7 broadcast_in_dim.48
  9.1 9.4 %all-to-all-start = ((f32[32,1,512]{2,1,0:T(1,128)}), f32[32,1,512]{2,1,0:T(1,128)S(1)}, u32[]{:S(2)}, u32[]{:S(2)}) async-start(f32[32,1,512]{2,1,0:T(1,128)} %broadcast_in_dim.48), calls=%async_computation | async-start | bytes 131072 | tf_op jit(solution)/shard_map/all_to_all | solution.py:17
  18.5 0.0 reduce-scatter.2.cloned.1.call-start
  18.5 0.7 and_select_fusion.1
  19.2 0.1 iota_add_fusion
  19.3 0.1 compare_and_fusion
  19.4 6.4 copy.61
  25.8 10.3 %gather_fusion = bf16[2048,512]{1,0:T(8,128)(2,1)S(1)} fusion(bf16[512,4096]{0,1:T(8,128)(2,1)} %copy.61, s32[2048]{0:T(1024)S(1)} %broadcast_clamp_fusion), kind=kCustom, calls=%fused_computation | custom fusion | bytes 4202496 | tf_op jit(solution)/shard_map/jit(_take)/gather | solution.py:81
  36.1 0.0 copy-start.4
  36.1 0.0 copy-start.5
  36.1 0.0 copy-start.2
  36.1 0.0 copy-start.9
  36.1 1.6 select_bitcast_fusion
  37.7 0.1 copy.62
  37.9 0.1 copy.63
  38.0 0.0 all-to-all-done
  38.0 0.1 reduce_sum.46
  38.1 0.0 copy-done.2
  38.1 0.0 copy-done.9
  38.1 5.5 fusion.1
  43.7 0.0 reduce-scatter.2.cloned.1.call-update
  43.7 0.0 copy-start.7
  43.7 0.0 copy-start.8
  43.7 11.8 %gather_fusion.1 = f32[2048]{0:T(1024)S(1)} fusion(f32[4096]{0:T(1024)S(1)} %copy-done, s32[2048]{0:T(1024)S(1)} %broadcast_clamp_fusion), kind=kCustom, calls=%fused_computation.1 | custom fusion | bytes 24576 | tf_op jit(solution)/shard_map/jit(_take)/gather | solution.py:82
  55.6 0.1 iota_compare_fusion
  55.7 0.1 broadcast_select_fusion
  55.8 0.1 multiply_cosine_fusion
  55.9 160.1 %reduce-scatter.2.cloned.1.call-done = f32[16,2560]{1,0:T(8,128)} async-done(((f32[512,2560]{1,0:T(8,128)}), f32[16,2560]{1,0:T(8,128)}) %reduce-scatter.2.cloned.1.call-update) | async-done | bytes 163856 | tf_op jit(solution)/shard_map/reduce_scatter | solution.py:85
  216.0 0.8 slice_multiply_fusion.1
  216.7 0.1 subtract_convert_fusion.1
  216.8 0.1 pad_maximum_fusion.1
  217.0 0.9 broadcast_in_dim.51
  217.8 7.7 %all-to-all-start.1 = ((bf16[32,16,512]{2,1,0:T(8,128)(2,1)}), bf16[32,16,512]{2,1,0:T(8,128)(2,1)S(1)}, u32[]{:S(2)}, u32[]{:S(2)}) async-start(bf16[32,16,512]{2,1,0:T(8,128)(2,1)} %broadcast_in_dim.51), calls=%async_computation.2 | async-start | bytes 1048576 | tf_op jit(solution)/shard_map/all_to_all | solution.py:17
  225.5 0.9 fusion.36
  226.4 0.1 fusion.50
  226.5 0.1 subtract_convert_fusion
  226.6 11.9 %all-to-all-done.1 = bf16[32,16,512]{2,1,0:T(8,128)(2,1)S(1)} async-done(((bf16[32,16,512]{2,1,0:T(8,128)(2,1)}), bf16[32,16,512]{2,1,0:T(8,128)(2,1)S(1)}, u32[]{:S(2)}, u32[]{:S(2)}) %all-to-all-start.1) | async-done | bytes 524320 | tf_op jit(solution)/shard_map/all_to_all | solution.py:17
  238.6 0.5 fusion.11
  239.1 0.5 fusion.10
  239.7 0.6 fusion.51
  240.3 0.4 fusion.23
  240.6 1.6 broadcast_in_dim.84
  242.2 6.2 all-to-all-start.2
  248.4 0.0 copy-start.10
  248.4 10.3 %gather_fusion.2 = bf16[2048,512]{1,0:T(8,128)(2,1)S(1)} fusion(bf16[4096,512]{1,0:T(8,128)(2,1)} %param.20, s32[2048]{0:T(1024)S(1)} %broadcast_clamp_fusion), kind=kCustom, calls=%fused_computation.2 | custom fusion | bytes 4202496 | tf_op jit(solution)/shard_map/jit(_take)/gather | solution.py:125
  258.7 7.9 %all-to-all-done.2 = bf16[32,16,2048]{2,1,0:T(8,128)(2,1)} async-done(((bf16[32,16,2048]{2,1,0:T(8,128)(2,1)}), bf16[32,16,2048]{2,1,0:T(8,128)(2,1)}, u32[]{:S(2)}, u32[]{:S(2)}) %all-to-all-start.2) | async-done | bytes 2097184 | tf_op jit(solution)/shard_map/all_to_all | solution.py:17
  266.6 3.1 fusion.24
  269.7 13.8 %all_to_all.64 = f32[32,1,512]{2,1,0:T(1,128)S(1)} all-to-all(f32[32,1,512]{2,1,0:T(1,128)S(1)} %broadcast_in_dim.87), channel_id=1, replica_groups=mesh['seq'=4,'fsdp'=32] {'fsdp'}, dimensions={0} | all-to-all | bytes 131072 | tf_op jit(solution)/shard_map/all_to_all | solution.py:17
  283.5 0.1 reduce_sum.49
  283.5 0.2 fusion.26
  283.7 13.9 %all_to_all.65 = bf16[32,16,512]{2,1,0:T(8,128)(2,1)S(1)} all-to-all(bf16[32,16,512]{2,1,0:T(8,128)(2,1)S(1)} %bitcast.50), channel_id=1, replica_groups=mesh['seq'=4,'fsdp'=32] {'fsdp'}, dimensions={0} | all-to-all | bytes 1048576 | tf_op jit(solution)/shard_map/all_to_all | solution.py:140
  297.6 0.3 copy.71
  297.9 0.4 all_to_all.52
  298.3 0.3 copy.72
  298.6 11.8 %all_to_all.66 = bf16[16,4,4096]{2,0,1:T(8,128)(2,1)S(1)} all-to-all(bf16[16,4,4096]{2,0,1:T(8,128)(2,1)S(1)} %copy.72), channel_id=1, replica_groups=mesh['seq'=4,'fsdp'=32] {'seq'}, dimensions={1} | all-to-all | bytes 1048576 | tf_op jit(solution)/shard_map/all_to_all | solution.py:139
  310.4 0.2 broadcast_in_dim.88
  310.6 29.6 %all_to_all.67 = bf16[4,512,512]{2,1,0:T(8,128)(2,1)S(1)} all-to-all(bf16[4,512,512]{2,1,0:T(8,128)(2,1)S(1)} %broadcast_in_dim.88), channel_id=1, replica_groups=mesh['seq'=4,'fsdp'=32] {'seq'}, dimensions={0} | all-to-all | bytes 4194304 | tf_op jit(solution)/shard_map/all_to_all | solution.py:17
  340.2 5.9 stack.5
  346.1 6.5 all-to-all-start.7
  352.6 1.6 copy.70
  354.2 280.9 %all-to-all-done.7 = bf16[32,64,4096]{2,1,0:T(8,128)(2,1)} async-done(((bf16[32,64,4096]{2,1,0:T(8,128)(2,1)}), bf16[32,64,4096]{2,1,0:T(8,128)(2,1)}, u32[]{:S(2)}, u32[]{:S(2)}) %all-to-all-start.7) | async-done | bytes 16777248 | tf_op jit(solution)/shard_map/all_to_all | solution.py:147
  635.2 15.2 %convolution_multiply_fusion = f32[512,4096]{1,0:T(8,128)} fusion(bf16[2048,512]{1,0:T(8,128)(2,1)} %bitcast.52, bf16[2048,4096]{1,0:T(8,128)(2,1)} %bitcast.17), kind=kOutput, calls=%fused_computation.4 | convolution fusion | flops 8592031744 | bytes 27262976 | tf_op jit(solution)/shard_map/dot_general | solution.py:149
  (30 shorter events, 0.3 us)
Async XLA Ops:
  7.2 36.5 %copy-start = (f32[4096]{0:T(1024)S(1)}, f32[4096]{0:T(1024)}, u32[]{:S(2)}) copy-start(f32[4096]{0:T(1024)} %param.15) | copy-start | bytes 49156
  9.1 28.9 %all-to-all-start = ((f32[32,1,512]{2,1,0:T(1,128)}), f32[32,1,512]{2,1,0:T(1,128)S(1)}, u32[]{:S(2)}, u32[]{:S(2)}) async-start(f32[32,1,512]{2,1,0:T(1,128)} %broadcast_in_dim.48), calls=%async_computation | async-start | bytes 131072 | tf_op jit(solution)/shard_map/all_to_all | solution.py:17
  18.5 197.5 %reduce-scatter.2.cloned.1.call-start = ((), (), s32[]{:S(2)}) async-start(), calls=%async_computation.9 | async-start | bytes 5406720 | tf_op jit(solution)/shard_map/reduce_scatter | solution.py:85
  36.1 1.6 copy-start.4
  36.1 1.8 copy-start.5
  36.1 2.0 copy-start.2
  36.1 2.0 copy-start.9
  43.7 11.9 %copy-start.7 = (f32[256]{0:T(256)S(1)}, f32[256]{0:T(256)}, u32[]{:S(2)}) copy-start(f32[256]{0:T(256)} %param.19) | copy-start | bytes 3076
  43.7 11.9 %copy-start.8 = (f32[256]{0:T(256)S(1)}, f32[256]{0:T(256)}, u32[]{:S(2)}) copy-start(f32[256]{0:T(256)} %param.17) | copy-start | bytes 3076
  217.8 20.7 %all-to-all-start.1 = ((bf16[32,16,512]{2,1,0:T(8,128)(2,1)}), bf16[32,16,512]{2,1,0:T(8,128)(2,1)S(1)}, u32[]{:S(2)}, u32[]{:S(2)}) async-start(bf16[32,16,512]{2,1,0:T(8,128)(2,1)} %broadcast_in_dim.51), calls=%async_computation.2 | async-start | bytes 1048576 | tf_op jit(solution)/shard_map/all_to_all | solution.py:17
  242.2 24.4 %all-to-all-start.2 = ((bf16[32,16,2048]{2,1,0:T(8,128)(2,1)}), bf16[32,16,2048]{2,1,0:T(8,128)(2,1)}, u32[]{:S(2)}, u32[]{:S(2)}) async-start(bf16[32,16,2048]{2,1,0:T(8,128)(2,1)} %broadcast_in_dim.84), calls=%async_computation.3 | async-start | bytes 4194304 | tf_op jit(solution)/shard_map/all_to_all | solution.py:17
  248.4 18.2 %copy-start.10 = (f32[512]{0:T(512)S(1)}, f32[512]{0:T(512)}, u32[]{:S(2)}) copy-start(f32[512]{0:T(512)} %param.21) | copy-start | bytes 6148
  266.6 16.9 %copy-start.6 = (f32[512]{0:T(512)S(1)}, f32[512]{0:T(512)}, u32[]{:S(2)}) copy-start(f32[512]{0:T(512)} %param.22) | copy-start | bytes 6148
  269.6 28.7 %copy-start.3 = (bf16[512,512]{1,0:T(8,128)(2,1)}, bf16[512,512]{1,0:T(8,128)(2,1)S(1)}, u32[]{:S(2)}) copy-start(bf16[512,512]{1,0:T(8,128)(2,1)S(1)} %get-tuple-element.17) | copy-start | bytes 1572868
  346.1 289.0 %all-to-all-start.7 = ((bf16[32,64,4096]{2,1,0:T(8,128)(2,1)}), bf16[32,64,4096]{2,1,0:T(8,128)(2,1)}, u32[]{:S(2)}, u32[]{:S(2)}) async-start(bf16[32,64,4096]{2,1,0:T(8,128)(2,1)} %stack.5), calls=%async_computation.8 | async-start | bytes 33554432 | tf_op jit(solution)/shard_map/all_to_all | solution.py:147
  635.2 15.2 %copy-start.1 = (f32[4096]{0:T(1024)S(1)}, f32[4096]{0:T(1024)}, u32[]{:S(2)}) copy-start(f32[4096]{0:T(1024)} %param.15) | copy-start | bytes 49156
Sparse Core Ops, SparseCore 0:
  43.8 172.1 reduce-scatter.1
